TPU v7x, 32 devices: a whole 2x2x4 slice. The times are simulated.
32 devices in a mesh: rep: 4 (over x, core), shard: 8 (over z, y).
Axes of the slice: x: 2, y: 2, z: 4, core: 2. Of those that a mesh axis runs over, the one named last changes fastest.
Arguments:
- block_input: bfloat16 [16384, 2048], P(('rep', 'shard')), may hold values from -6 to 6
- cotangent: bfloat16 [16384, 2048], P(('rep', 'shard')), may hold values from -6 to 6
- seq_lengths: int32 [4], replicated, may hold values from 1024 to 4096, as said below
- slot_order: int32 [4], replicated, may hold values from 0 to 3, each once
- norm_gain: bfloat16 [2048], P('shard'), may hold values from 0.5 to 1.5
- in_proj: bfloat16 [2048, 8192], P('shard'), may hold values from -0.125 to 0.125
- conv_weight: bfloat16 [4, 4096], P(None, 'shard'), may hold values from -3 to 3
- conv_bias: bfloat16 [4096], P('shard'), may hold values from -3 to 3
- x_proj: bfloat16 [4096, 160], P('shard'), may hold values from -0.09375 to 0.09375
- dt_proj: bfloat16 [128, 4096], P(None, 'shard'), may hold values from -0.5 to 0.5
- dt_bias: bfloat16 [4096], P('shard'), may hold values from -7 to -3
- a_log: bfloat16 [16, 4096], P(None, 'shard'), may hold values from -4 to 0.5
- d_skip: bfloat16 [4096], P('shard'), may hold values from 0.5 to 1.5
- out_proj: bfloat16 [4096, 2048], P('shard'), may hold values from -0.375 to 0.375
Outputs:
- activations: bfloat16 [16384, 2048], P(('rep', 'shard'))
- input_grad: float32 [16384, 2048], P(('rep', 'shard'))
- grad_norm_gain: float32 [2048], P('shard')
- grad_in_proj: float32 [2048, 8192], P('shard')
- grad_conv_weight: float32 [4, 4096], P(None, 'shard')
- grad_conv_bias: float32 [4096], P('shard')
- grad_x_proj: float32 [4096, 160], P('shard')
- grad_dt_proj: float32 [128, 4096], P(None, 'shard')
- grad_dt_bias: float32 [4096], P('shard')
- grad_a_log: float32 [16, 4096], P(None, 'shard')
- grad_d_skip: float32 [4096], P('shard')
- grad_out_proj: float32 [4096, 2048], P('shard')
Inputs may be any that keep to these rules, and one draw needn't show every extreme that they name: `seq_lengths`: each sequence has 1024 to 4096 tokens; one sequence has exactly 4096 and one exactly 1024.
All inputs are finite; a program needn't handle non-finite values.
Results may differ from a plain program's by a relative error of at most 0.015.
Values may be sent and summed in bfloat16 or wider, within the bound.
A program may use at most 384 MiB of HBM per device.

v0:
```python
from functools import partial
import jax
import jax.numpy as jnp
from jax import lax
from jax.sharding import PartitionSpec as P

STRETCH = 32
EPSILON = 1e-05
HIGHEST = lax.Precision.HIGHEST


def shifted(value, axis, steps):
    count = lax.axis_size(axis)
    first, last = (max(0, -steps), min(count, count - steps))
    return lax.ppermute(value, axis, [(source, source + steps) for source in range(first, last)])


def prefix(value, axis, combine, identity, reverse):
    devices, mine = (lax.axis_size(axis), lax.axis_index(axis))
    everything = jax.tree.map(lambda part: lax.all_gather(part, axis), value)
    start = jax.tree.map(
        lambda part, zero: jnp.broadcast_to(jnp.asarray(zero, part.dtype), part.shape),
        value,
        identity,
    )

    def lap(k, before):
        at = devices - 1 - k if reverse else k
        reached = at > mine if reverse else at < mine
        new = combine(before, jax.tree.map(lambda part: part[at], everything))
        return jax.tree.map(lambda a, b: jnp.where(reached, a, b), new, before)

    return lax.fori_loop(0, devices, lap, start)


def split_blocks(values, width):
    return values.reshape((values.shape[0] // width, width) + values.shape[1:])


def combine_maps(earlier, later):
    return (earlier[0] * later[0], later[0] * earlier[1] + later[1])


def contract_rows(left, right):
    return lax.dot_general(
        left, right, (((0,), (0,)), ((), ())), preferred_element_type=jnp.float32
    )


def contract_cols(left, right):
    return lax.dot_general(
        left, right, (((1,), (1,)), ((), ())), preferred_element_type=jnp.float32
    )


def selective(step_size, conv_out, input_coeff, output_coeff, rates, start_state):

    @jax.checkpoint
    def selective_block_step(state, pieces):
        step_block, conv_block, input_block, output_block = pieces
        running = jnp.cumsum(step_block, axis=0)
        exponent = rates[None, :, :] * running[:, None, :]
        feeding = (step_block * conv_block)[:, None, :] * input_block[:, :, None]
        summed = jnp.cumsum(jnp.exp(-exponent) * feeding, axis=0)
        states = jnp.exp(exponent) * (state[None, :, :] + summed)
        emitted = jnp.einsum("qn,qne->qe", output_block, states, precision=HIGHEST)
        return (states[-1], emitted)

    final_state, emitted = lax.scan(
        selective_block_step,
        start_state,
        (
            split_blocks(step_size, STRETCH),
            split_blocks(conv_out, STRETCH),
            split_blocks(input_coeff, STRETCH),
            split_blocks(output_coeff, STRETCH),
        ),
    )
    return (emitted.reshape(step_size.shape), final_state)


def end_state(step_size, conv_out, input_coeff, rates):

    def end_block_step(state, pieces):
        step_block, conv_block, input_block = pieces
        running = jnp.cumsum(step_block, axis=0)
        total = running[-1]
        weighting = jnp.exp(rates[None, :, :] * (total[None, None, :] - running[:, None, :]))
        feeding = (step_block * conv_block)[:, None, :] * input_block[:, :, None]
        return (
            jnp.exp(rates * total[None, :]) * state + jnp.sum(weighting * feeding, axis=0),
            None,
        )

    start_state = jnp.zeros(rates.shape, jnp.float32)
    final_state, unused = lax.scan(
        end_block_step,
        start_state,
        (
            split_blocks(step_size, STRETCH),
            split_blocks(conv_out, STRETCH),
            split_blocks(input_coeff, STRETCH),
        ),
    )
    return final_state


def start_weight(step_size, output_coeff, g_scanned, rates):

    def start_block_step(carry, pieces):
        total, before = carry
        step_block, output_block, grad_block = pieces
        running = before[None, :] + jnp.cumsum(step_block, axis=0)
        weighting = jnp.exp(rates[None, :, :] * running[:, None, :])
        total = total + jnp.sum(
            weighting * output_block[:, :, None] * grad_block[:, None, :], axis=0
        )
        return ((total, running[-1]), None)

    initial = (jnp.zeros(rates.shape, jnp.float32), jnp.zeros((rates.shape[1],), jnp.float32))
    result, unused = lax.scan(
        start_block_step,
        initial,
        (
            split_blocks(step_size, STRETCH),
            split_blocks(output_coeff, STRETCH),
            split_blocks(g_scanned, STRETCH),
        ),
    )
    return result[0]


def conv_local(edge_rows, conv_in, taps, bias_row, keep_prev):
    tok_rows = conv_in.shape[0]
    padded = jnp.concatenate([edge_rows * keep_prev, conv_in], axis=0)
    total = bias_row[None, :]
    for offset in range(taps.shape[0]):
        total = total + taps[offset][None, :] * padded[offset : offset + tok_rows]
    return jax.nn.silu(total)


def mixer_scan(
    step_size, conv_low, input_coeff, output_coeff, log_rates, skip_gain, gate_in, start_state
):
    rates = -jnp.exp(log_rates)
    scanned, final_state = selective(
        step_size, conv_low, input_coeff, output_coeff, rates, start_state
    )
    scanned = scanned + skip_gain[None, :] * conv_low
    return (scanned * jax.nn.silu(gate_in), final_state)


def on_device(
    block_input,
    cotangent,
    seq_lengths,
    slot_order,
    norm_gain,
    in_proj,
    conv_weight,
    conv_bias,
    x_proj,
    dt_proj,
    dt_bias,
    a_log,
    d_skip,
    out_proj,
):
    n_shard = lax.axis_size("shard")
    tok_rows = block_input.shape[0]
    inner_width = conv_bias.shape[0] * n_shard
    rank_width = dt_proj.shape[0]
    state_width = a_log.shape[0]
    kernel_taps = conv_weight.shape[0]
    span_devs = max(1, min(n_shard, 4096 // tok_rows))
    shard_at = lax.axis_index("shard")
    rep_at = lax.axis_index("rep")
    in_slot = shard_at % span_devs
    keep_prev = (in_slot != 0).astype(jnp.float32)
    slot_at = (rep_at * n_shard + shard_at) // span_devs
    slot_len = jnp.sum(jnp.where(slot_order == slot_at, seq_lengths, 0))
    places = in_slot * tok_rows + jnp.arange(tok_rows, dtype=jnp.int32)
    valid_rows = (places < slot_len).astype(jnp.float32)[:, None]
    gathered = (
        lax.all_gather(norm_gain, "shard", axis=0, tiled=True),
        lax.all_gather(in_proj, "shard", axis=0, tiled=True),
        lax.all_gather(conv_weight, "shard", axis=1, tiled=True),
        lax.all_gather(conv_bias, "shard", axis=0, tiled=True),
        lax.all_gather(x_proj, "shard", axis=0, tiled=True),
        lax.all_gather(dt_proj, "shard", axis=1, tiled=True),
        lax.all_gather(dt_bias, "shard", axis=0, tiled=True),
        lax.all_gather(a_log, "shard", axis=1, tiled=True),
        lax.all_gather(d_skip, "shard", axis=0, tiled=True),
        lax.all_gather(out_proj, "shard", axis=0, tiled=True),
    )
    (
        gain_all,
        in_all,
        taps_all,
        bias_all,
        xproj_all,
        dtproj_all,
        dtbias_all,
        alog_all,
        skip_all,
        out_all,
    ) = gathered
    gain_f = gain_all.astype(jnp.float32)
    input_f = block_input.astype(jnp.float32)
    scale = lax.rsqrt(jnp.mean(input_f * input_f, axis=1, keepdims=True) + EPSILON)
    normed = (input_f * scale * gain_f[None, :]).astype(jnp.bfloat16)
    mixed_in = jnp.dot(normed, in_all, preferred_element_type=jnp.float32)
    conv_in = mixed_in[:, :inner_width].astype(jnp.bfloat16)
    gate_in = mixed_in[:, inner_width:]
    edge_rows = shifted(conv_in[tok_rows - (kernel_taps - 1) :], "shard", 1)
    conv_f, conv_back = jax.vjp(
        partial(conv_local, keep_prev=keep_prev),
        edge_rows.astype(jnp.float32),
        conv_in.astype(jnp.float32),
        taps_all.astype(jnp.float32),
        bias_all.astype(jnp.float32),
    )
    conv_out = conv_f.astype(jnp.bfloat16)
    conv_low = conv_out.astype(jnp.float32)
    projected = jnp.dot(conv_out, xproj_all, preferred_element_type=jnp.float32)
    step_low = projected[:, :rank_width].astype(jnp.bfloat16)
    input_coeff = projected[:, rank_width : rank_width + state_width]
    output_coeff = projected[:, rank_width + state_width :]
    step_pre = (
        jnp.dot(step_low, dtproj_all, preferred_element_type=jnp.float32)
        + dtbias_all.astype(jnp.float32)[None, :]
    )
    step_size = jax.nn.softplus(step_pre)
    log_rates = alog_all.astype(jnp.float32)
    rates = -jnp.exp(log_rates)
    local_end = end_state(step_size, conv_low, input_coeff, rates)
    through = jnp.exp(rates * jnp.sum(step_size, axis=0)[None, :])
    carried = prefix(
        (through * keep_prev, local_end),
        "shard",
        combine_maps,
        (jnp.ones_like(through), jnp.zeros_like(local_end)),
        False,
    )
    start_state = carried[1] * keep_prev
    mixer_out, scan_back = jax.vjp(
        mixer_scan,
        step_size,
        conv_low,
        input_coeff,
        output_coeff,
        log_rates,
        skip_all.astype(jnp.float32),
        gate_in,
        start_state,
    )
    gated = mixer_out[0].astype(jnp.bfloat16)
    branch = jnp.dot(gated, out_all, preferred_element_type=jnp.float32)
    activations = (input_f + valid_rows * branch).astype(jnp.bfloat16)
    in_back, xproj_back, dtproj_back, out_back = (
        lax.all_gather(in_proj, "shard", axis=0, tiled=True),
        lax.all_gather(x_proj, "shard", axis=0, tiled=True),
        lax.all_gather(dt_proj, "shard", axis=1, tiled=True),
        lax.all_gather(out_proj, "shard", axis=0, tiled=True),
    )
    cot_f = cotangent.astype(jnp.float32)
    back_rows = (cot_f * valid_rows).astype(jnp.bfloat16)
    grad_out_proj = contract_rows(gated, back_rows)
    g_gated = contract_cols(back_rows, out_back)
    g_scanned = g_gated * jax.nn.silu(gate_in)
    local_grad = start_weight(step_size, output_coeff, g_scanned, rates)
    returned = prefix(
        (through * keep_prev, local_grad * keep_prev),
        "shard",
        combine_maps,
        (jnp.ones_like(through), jnp.zeros_like(local_grad)),
        True,
    )
    end_grad = returned[1]
    (
        g_step,
        g_conv_scan,
        g_input_coeff,
        g_output_coeff,
        grad_a_log,
        grad_d_skip,
        g_gate_in,
        unused_grad,
    ) = scan_back((g_gated, end_grad))
    g_pre_step = g_step * jax.nn.sigmoid(step_pre)
    grad_dt_bias = jnp.sum(g_pre_step, axis=0)
    g_lin = g_pre_step.astype(jnp.bfloat16)
    grad_dt_proj = contract_rows(step_low, g_lin)
    g_step_low = contract_cols(g_lin, dtproj_back)
    g_projected = jnp.concatenate([g_step_low, g_input_coeff, g_output_coeff], axis=1).astype(
        jnp.bfloat16
    )
    grad_x_proj = contract_rows(conv_out, g_projected)
    g_conv_out = contract_cols(g_projected, xproj_back) + g_conv_scan
    g_edge, g_conv_in, grad_conv_weight, grad_conv_bias = conv_back(g_conv_out)
    from_next = shifted(g_edge.astype(jnp.bfloat16), "shard", -1).astype(g_edge.dtype)
    split_at = tok_rows - (kernel_taps - 1)
    g_conv_in = jnp.concatenate([g_conv_in[:split_at], g_conv_in[split_at:] + from_next], axis=0)
    g_mixed = jnp.concatenate([g_conv_in, g_gate_in], axis=1).astype(jnp.bfloat16)
    grad_in_proj = contract_rows(normed, g_mixed)
    g_normed = contract_cols(g_mixed, in_back)
    grad_norm_gain = jnp.sum(g_normed * input_f * scale, axis=0)
    g_hat = g_normed * gain_f[None, :]
    input_grad = (
        cot_f
        + scale * g_hat
        - input_f * (scale * scale * scale) * jnp.mean(g_hat * input_f, axis=1, keepdims=True)
    )
    shares = (
        lax.psum_scatter(
            grad_norm_gain.astype(jnp.bfloat16), "shard", scatter_dimension=0, tiled=True
        ).astype(jnp.float32),
        lax.psum_scatter(
            grad_in_proj.astype(jnp.bfloat16), "shard", scatter_dimension=0, tiled=True
        ).astype(jnp.float32),
        lax.psum_scatter(
            grad_conv_weight.astype(jnp.bfloat16), "shard", scatter_dimension=1, tiled=True
        ).astype(jnp.float32),
        lax.psum_scatter(
            grad_conv_bias.astype(jnp.bfloat16), "shard", scatter_dimension=0, tiled=True
        ).astype(jnp.float32),
        lax.psum_scatter(
            grad_x_proj.astype(jnp.bfloat16), "shard", scatter_dimension=0, tiled=True
        ).astype(jnp.float32),
        lax.psum_scatter(
            grad_dt_proj.astype(jnp.bfloat16), "shard", scatter_dimension=1, tiled=True
        ).astype(jnp.float32),
        lax.psum_scatter(
            grad_dt_bias.astype(jnp.bfloat16), "shard", scatter_dimension=0, tiled=True
        ).astype(jnp.float32),
        lax.psum_scatter(
            grad_a_log.astype(jnp.bfloat16), "shard", scatter_dimension=1, tiled=True
        ).astype(jnp.float32),
        lax.psum_scatter(
            grad_d_skip.astype(jnp.bfloat16), "shard", scatter_dimension=0, tiled=True
        ).astype(jnp.float32),
        lax.psum_scatter(
            grad_out_proj.astype(jnp.bfloat16), "shard", scatter_dimension=0, tiled=True
        ).astype(jnp.float32),
    )
    totals = (
        lax.psum(shares[0].astype(jnp.bfloat16), "rep").astype(jnp.float32),
        lax.psum(shares[1].astype(jnp.bfloat16), "rep").astype(jnp.float32),
        lax.psum(shares[2].astype(jnp.bfloat16), "rep").astype(jnp.float32),
        lax.psum(shares[3].astype(jnp.bfloat16), "rep").astype(jnp.float32),
        lax.psum(shares[4].astype(jnp.bfloat16), "rep").astype(jnp.float32),
        lax.psum(shares[5].astype(jnp.bfloat16), "rep").astype(jnp.float32),
        lax.psum(shares[6].astype(jnp.bfloat16), "rep").astype(jnp.float32),
        lax.psum(shares[7].astype(jnp.bfloat16), "rep").astype(jnp.float32),
        lax.psum(shares[8].astype(jnp.bfloat16), "rep").astype(jnp.float32),
        lax.psum(shares[9].astype(jnp.bfloat16), "rep").astype(jnp.float32),
    )
    return (
        activations,
        input_grad,
        totals[0],
        totals[1],
        totals[2],
        totals[3],
        totals[4],
        totals[5],
        totals[6],
        totals[7],
        totals[8],
        totals[9],
    )


def solution(mesh):
    in_specs = (
        P(("rep", "shard"), None),
        P(("rep", "shard"), None),
        P(),
        P(),
        P("shard"),
        P("shard", None),
        P(None, "shard"),
        P("shard"),
        P("shard", None),
        P(None, "shard"),
        P("shard"),
        P(None, "shard"),
        P("shard"),
        P("shard", None),
    )
    out_specs = (
        P(("rep", "shard"), None),
        P(("rep", "shard"), None),
        P("shard"),
        P("shard", None),
        P(None, "shard"),
        P("shard"),
        P("shard", None),
        P(None, "shard"),
        P("shard"),
        P(None, "shard"),
        P("shard"),
        P("shard", None),
    )
    return jax.shard_map(
        on_device, mesh=mesh, in_specs=in_specs, out_specs=out_specs, check_vma=False
    )
```

profile of v0, /device:TPU:0, one launch (start us, length us, event | category | flops | bytes accessed | tf_op | source)
XLA Modules:
  0.0 3641.3 jit_solution(2845981846549221471)
XLA Ops:
  10.8 62.7 %all-gather.4 = bf16[8,1,256]{2,1,0:T(2,128)(2,1)S(1)} all-gather(bf16[1,1,256]{2,1,0:T(2,128)(2,1)S(1)} %reshape.226), channel_id=1, replica_groups=mesh['rep'=4,'shard'=8] {'shard'}, dimensions={0}, use_global_device_ids=true | all-gather | bytes 4608 | tf_op jit(solution)/shard_map/all_gather | solution.py:185
  76.2 44.4 %all_gather.56 = bf16[4,4096]{1,0:T(4,128)(2,1)S(1)} all-gather(bf16[4,512]{1,0:T(4,128)(2,1)S(1)} %copy-done.41), channel_id=1, replica_groups=mesh['rep'=4,'shard'=8] {'shard'}, dimensions={1}, use_global_device_ids=true | all-gather | bytes 36864 | tf_op jit(solution)/shard_map/all_gather | solution.py:187
  120.7 43.0 %all-gather.3 = bf16[8,1,512]{2,1,0:T(2,128)(2,1)S(1)} all-gather(bf16[1,1,512]{2,1,0:T(2,128)(2,1)S(1)} %reshape.224), channel_id=1, replica_groups=mesh['rep'=4,'shard'=8] {'shard'}, dimensions={0}, use_global_device_ids=true | all-gather | bytes 9216 | tf_op jit(solution)/shard_map/all_gather | solution.py:188
  163.8 47.1 %all_gather.54 = bf16[16,4096]{1,0:T(8,128)(2,1)S(1)} all-gather(bf16[16,512]{1,0:T(8,128)(2,1)S(1)} %copy-done.28), channel_id=1, replica_groups=mesh['rep'=4,'shard'=8] {'shard'}, dimensions={1}, use_global_device_ids=true | all-gather | bytes 147456 | tf_op jit(solution)/shard_map/all_gather | solution.py:192
  210.9 41.2 %all-gather.5 = bf16[8,1,512]{2,1,0:T(2,128)(2,1)S(1)} all-gather(bf16[1,1,512]{2,1,0:T(2,128)(2,1)S(1)} %reshape.228), channel_id=1, replica_groups=mesh['rep'=4,'shard'=8] {'shard'}, dimensions={0}, use_global_device_ids=true | all-gather | bytes 9216 | tf_op jit(solution)/shard_map/all_gather | solution.py:191
  253.5 400.3 %all-gather.15.cloned.1.call-done = bf16[2048,8192]{1,0:T(8,128)(2,1)} async-done(((bf16[256,8192]{1,0:T(8,128)(2,1)}), bf16[2048,8192]{1,0:T(8,128)(2,1)}) %all-gather.15.cloned.1.call-update) | async-done | bytes 33554448 | tf_op jit(solution)/shard_map/all_gather | solution.py:186
  653.8 27.6 fusion.92
  692.0 191.7 %all-gather.21.cloned.1.call-done = bf16[4096,2048]{1,0:T(8,128)(2,1)} async-done(((bf16[512,2048]{1,0:T(8,128)(2,1)}), bf16[4096,2048]{1,0:T(8,128)(2,1)}) %all-gather.21.cloned.1.call-update) | async-done | bytes 16777232 | tf_op jit(solution)/shard_map/all_gather | solution.py:194
  883.8 32.5 multiply_reduce_fusion.6
  929.7 35.5 all-gather.19.cloned.1.call-done
  982.8 78.1 %while.94 = (s32[]{:T(128)}, f32[16,4096]{1,0:T(8,128)S(1)}, f32[16,32,4096]{2,1,0:T(8,128)}, f32[16,4096]{1,0:T(8,128)S(1)}, f32[16,32,4096]{2,1,0:T(8,128)}, /...) while((s32[]{:T(128)}, f32[16,4096]{1,0:T(8,128)S(1)}, ...), condition=%wide.region_6.7_spmd.clone, body=%wide.region_3.6_spmd.clone.sunk | while | flops 12910595 | bytes 7415935 | solution.py:96
  1063.1 60.4 %while.96 = (s32[]{:T(128)}, f32[16,4096]{1,0:T(8,128)S(1)}, f32[4096]{0:T(1024)S(1)}, f32[16,4096]{1,0:T(8,128)S(1)}, f32[16,32,4096]{2,1,0:T(8,128)}, /*index=...) while((s32[]{:T(128)}, f32[16,4096]{1,0:T(8,128)S(1)}, ...), condition=%wide.region_16.17_spmd.clone, body=%wide.region_13.16_spmd.clone.sunk | while | flops 12648451 | bytes 6613123 | solution.py:121
  1139.0 276.5 %while.93 = (s32[]{:T(128)}, f32[16,4096]{1,0:T(8,128)S(1)}, f32[16,32,4096]{2,1,0:T(8,128)}, f32[16,16,4096]{2,1,0:T(8,128)}, f32[1,16,4096]{2,1,0:T(8,128)S(1)...) while((s32[]{:T(128)}, f32[16,4096]{1,0:T(8,128)S(1)}, ...), condition=%wide.region_12.13_spmd, body=%wide.region_9.12_spmd.sunk | while | flops 109051904 | bytes 58212524 | solution.py:69
  1434.9 962.9 %while.98 = (s32[]{:T(128)}, f32[16,4096]{1,0:T(8,128)}, f32[16,4096]{1,0:T(8,128)S(1)}, f32[16,32,4096]{2,1,0:T(8,128)}, f32[16,32,4096]{2,1,0:T(8,128)}, /*ind...) while((s32[]{:T(128)}, f32[16,4096]{1,0:T(8,128)}, ...), condition=%wide.region_29.30_spmd.clone, body=%wide.region_19.29_spmd.clone.sunk | while | flops 243269120 | bytes 81833296 | solution.py:69
  1445.9 15.1 fusion.135
  1506.0 15.1 fusion.135
  1566.2 15.1 fusion.135
  1626.3 15.1 fusion.135
  1686.5 15.1 fusion.135
  1746.6 15.1 fusion.135
  1927.1 15.1 fusion.135
  2167.7 15.1 fusion.135
  2348.1 15.1 fusion.135
  2409.4 26.3 all-gather.6
  2473.6 33.0 multiply_reduce_fusion.9
  2525.4 24.6 convolution_convert_fusion
  2569.8 254.5 %reduce-scatter.17.cloned.1.call-done = bf16[512,2048]{1,0:T(8,128)(2,1)} async-done(((bf16[4096,2048]{1,0:T(8,128)(2,1)}), bf16[512,2048]{1,0:T(8,128)(2,1)}) %reduce-scatter.17.cloned.1.call-update) | async-done | bytes 2097168 | tf_op jit(solution)/shard_map/reduce_scatter | solution.py:342
  2824.3 541.7 %reduce-scatter.9.cloned.1.call-done = bf16[256,8192]{1,0:T(8,128)(2,1)} async-done(((bf16[2048,8192]{1,0:T(8,128)(2,1)}), bf16[256,8192]{1,0:T(8,128)(2,1)}) %reduce-scatter.9.cloned.1.call-update) | async-done | bytes 4194320 | tf_op jit(solution)/shard_map/reduce_scatter | solution.py:318
  3366.1 25.3 fusion.61
  3391.4 35.5 all-reduce.13
  3434.2 63.6 %reduce-scatter.15.cloned.1.call-done = bf16[16,512]{1,0:T(8,128)(2,1)} async-done(((bf16[16,4096]{1,0:T(8,128)(2,1)}), bf16[16,512]{1,0:T(8,128)(2,1)}) %reduce-scatter.15.cloned.1.call-update) | async-done | bytes 16400 | tf_op jit(solution)/shard_map/reduce_scatter | solution.py:336
  3512.2 111.5 %all-reduce.18.cloned.1.call-done = (bf16[256,8192]{1,0:T(8,128)(2,1)}, bf16[512,160]{0,1:T(8,128)(2,1)}, bf16[128,512]{1,0:T(8,128)(2,1)}, bf16[512,2048]{1,0:T(8,128)(2,1)}) async-done(((bf16[256,8192]{1,0:T(8,128)(2,1)}, bf16[512,160]{0,1:T(8,128)(2,1)}, bf16[128,512]{1,0:T(8,128)(2,1)}, bf16[512,2048]{1,0:T(8,128)(2,1)}), (bf16[256,8192]{1,0:T(8,128)(2,1)}, bf16[512,160]{0,1:T(8,128)(2,1)}, ...) | async-done | bytes 6586384 | tf_op jit(solution)/shard_map/psum | solution.py:348
  (1111 shorter events, 1462.6 us)
Async XLA Ops:
  7.2 156.6 %copy-start.28 = (bf16[16,512]{1,0:T(8,128)(2,1)S(1)}, bf16[16,512]{1,0:T(8,128)(2,1)}, u32[]{:S(2)}) copy-start(bf16[16,512]{1,0:T(8,128)(2,1)} %param.37) | copy-start | bytes 49156
  7.2 203.7 %copy-start.45 = (bf16[512]{0:T(512)(128)(2,1)S(1)}, bf16[512]{0:T(512)(128)(2,1)}, u32[]{:S(2)}) copy-start(bf16[512]{0:T(512)(128)(2,1)} %param.36) | copy-start | bytes 3076
  7.2 244.9 %copy-start.47 = (s32[4]{0:T(128)S(1)}, s32[4]{0:T(128)}, u32[]{:S(2)}) copy-start(s32[4]{0:T(128)} %param.28) | copy-start | bytes 52
  7.2 244.9 %copy-start.48 = (s32[4]{0:T(128)S(1)}, s32[4]{0:T(128)}, u32[]{:S(2)}) copy-start(s32[4]{0:T(128)} %param.29) | copy-start | bytes 52
  7.2 646.6 %all-gather.15.cloned.1.call-start = ((), (), s32[]{:S(2)}) async-start(), calls=%async_computation.6 | async-start | bytes 37748736 | tf_op jit(solution)/shard_map/all_gather | solution.py:186
  8.0 875.8 %all-gather.21.cloned.1.call-start = ((), (), s32[]{:S(2)}) async-start(), calls=%async_computation.9 | async-start | bytes 18874368 | tf_op jit(solution)/shard_map/all_gather | solution.py:194
  8.7 916.8 %all-gather.17.cloned.1.call-start = ((), (), s32[]{:S(2)}) async-start(), calls=%async_computation.7 | async-start | bytes 1474560 | tf_op jit(solution)/shard_map/all_gather | solution.py:189
  9.5 955.8 %all-gather.19.cloned.1.call-start = ((), (), s32[]{:S(2)}) async-start(), calls=%async_computation.8 | async-start | bytes 1179648 | tf_op jit(solution)/shard_map/all_gather | solution.py:190
  10.0 1114.5 %all-gather.23.cloned.1.call-start = ((), (), s32[]{:S(2)}) async-start(), calls=%async_computation.15 | async-start | bytes 2359296 | tf_op jit(solution)/shard_map/all_gather | solution.py:20
  73.5 607.9 %copy-start.26 = (f32[8,1,256]{2,1,0:T(1,128)}, f32[8,1,256]{2,1,0:T(1,128)S(1)}, u32[]{:S(2)}) copy-start(f32[8,1,256]{2,1,0:T(1,128)S(1)} %convert_element_type.193) | copy-start | bytes 24580
  76.2 605.2 %copy-start.39 = (f32[512]{0:T(512)}, f32[512]{0:T(512)S(1)}, u32[]{:S(2)}) copy-start(f32[512]{0:T(512)S(1)} %get-tuple-element.1084) | copy-start | bytes 6148
  120.6 763.1 %copy-start.29 = (f32[1,4096]{1,0:T(1,128)}, f32[1,4096]{1,0:T(1,128)S(1)}, u32[]{:S(2)}) copy-start(f32[1,4096]{1,0:T(1,128)S(1)} %get-tuple-element.1079) | copy-start | bytes 49156
  120.6 763.1 %copy-start.31 = (f32[1,4096]{1,0:T(1,128)}, f32[1,4096]{1,0:T(1,128)S(1)}, u32[]{:S(2)}) copy-start(f32[1,4096]{1,0:T(1,128)S(1)} %get-tuple-element.1080) | copy-start | bytes 49156
  120.6 763.1 %copy-start.33 = (f32[1,4096]{1,0:T(1,128)}, f32[1,4096]{1,0:T(1,128)S(1)}, u32[]{:S(2)}) copy-start(f32[1,4096]{1,0:T(1,128)S(1)} %get-tuple-element.1081) | copy-start | bytes 49156
  120.6 763.1 %copy-start.35 = (f32[1,4096]{1,0:T(1,128)}, f32[1,4096]{1,0:T(1,128)S(1)}, u32[]{:S(2)}) copy-start(f32[1,4096]{1,0:T(1,128)S(1)} %get-tuple-element.1082) | copy-start | bytes 49156
  210.9 764.4 %copy-start.12 = (bf16[16,4096]{1,0:T(8,128)(2,1)}, bf16[16,4096]{1,0:T(8,128)(2,1)S(1)}, u32[]{:S(2)}) copy-start(bf16[16,4096]{1,0:T(8,128)(2,1)S(1)} %all_gather.54) | copy-start | bytes 393220
  252.1 713.1 %copy-start.23 = (f32[8,1,512]{2,1,0:T(1,128)}, f32[8,1,512]{2,1,0:T(1,128)S(1)}, u32[]{:S(2)}) copy-start(f32[8,1,512]{2,1,0:T(1,128)S(1)} %convert_element_type.194) | copy-start | bytes 49156
  253.5 630.3 %copy-start.42 = (f32[512]{0:T(512)}, f32[512]{0:T(512)S(1)}, u32[]{:S(2)}) copy-start(f32[512]{0:T(512)S(1)} %fusion.81) | copy-start | bytes 6148
  682.3 9.7 collective-permute-start
  692.0 224.2 %copy-start.21 = (f32[3,4096]{1,0:T(4,128)}, f32[3,4096]{1,0:T(4,128)S(1)}, u32[]{:S(2)}) copy-start(f32[3,4096]{1,0:T(4,128)S(1)} %convert_multiply_fusion.6) | copy-start | bytes 147460
  976.1 148.4 %all-gather.25.cloned.1.call-start = ((), (), s32[]{:S(2)}) async-start(), calls=%async_computation.16 | async-start | bytes 2359296 | tf_op jit(solution)/shard_map/all_gather | solution.py:20
  1062.6 352.9 %all-gather.27.cloned.1.call-start = ((), (), s32[]{:S(2)}) async-start(), calls=%async_computation.17 | async-start | bytes 2359296 | tf_op jit(solution)/shard_map/all_gather | solution.py:20
  1124.4 1445.4 %reduce-scatter.13.cloned.1.call-start = ((), (), s32[]{:S(2)}) async-start(), calls=%async_computation.12 | async-start | bytes 1179648 | tf_op jit(solution)/shard_map/reduce_scatter | solution.py:330
  1139.0 276.5 %copy-start.2 = (f32[16,4096]{1,0:T(8,128)S(1)}, f32[16,4096]{1,0:T(8,128)}, u32[]{:S(2)}) copy-start(f32[16,4096]{1,0:T(8,128)} %custom-call.3) | copy-start | bytes 786436
  1434.9 963.0 %copy-start.24 = (f32[8,1,512]{2,1,0:T(1,128)S(1)}, f32[8,1,512]{2,1,0:T(1,128)}, u32[]{:S(2)}) copy-start(f32[8,1,512]{2,1,0:T(1,128)} %copy-done.23) | copy-start | bytes 49156
  2409.4 160.5 %reduce-scatter.11.cloned.1.call-start = ((), (), s32[]{:S(2)}) async-start(), calls=%async_computation.11 | async-start | bytes 1474560 | tf_op jit(solution)/shard_map/reduce_scatter | solution.py:327
  2443.9 380.4 %reduce-scatter.17.cloned.1.call-start = ((), (), s32[]{:S(2)}) async-start(), calls=%async_computation.14 | async-start | bytes 18874368 | tf_op jit(solution)/shard_map/reduce_scatter | solution.py:342
  2472.8 893.2 %reduce-scatter.9.cloned.1.call-start = ((), (), s32[]{:S(2)}) async-start(), calls=%async_computation.10 | async-start | bytes 37748736 | tf_op jit(solution)/shard_map/reduce_scatter | solution.py:318
  2507.7 15.0 collective-permute-start.1
  2550.1 883.1 %reduce-scatter.19.cloned.1.call-start = ((), (), s32[]{:S(2)}) async-start(), calls=%async_computation.18 | async-start | bytes 1179648
  2554.1 943.6 %reduce-scatter.15.cloned.1.call-start = ((), (), s32[]{:S(2)}) async-start(), calls=%async_computation.13 | async-start | bytes 147456 | tf_op jit(solution)/shard_map/reduce_scatter | solution.py:336
  2554.9 1068.8 %all-reduce.18.cloned.1.call-start = ((), (), s32[]{:S(2)}) async-start(), calls=%async_computation.19 | async-start | bytes 13172736 | tf_op jit(solution)/shard_map/psum | solution.py:348
  (110 other events, 1283.6 us)
Sparse Core Ops, SparseCore 0:
  9.6 644.1 all-gather.14
  655.9 227.7 all-gather.20
  885.8 39.7 all-gather.16
  927.5 37.7 all-gather.18
  976.2 48.0 all-gather.22
  1062.7 48.2 all-gather.24
  1124.6 48.2 all-gather.26
  2409.5 63.7 reduce-scatter.12
  2476.7 64.6 reduce-scatter.10
  2545.1 279.2 reduce-scatter.16
  2828.1 537.8 reduce-scatter.8
  3369.3 63.4 reduce-scatter.18
  3436.6 61.1 reduce-scatter.14
  3500.2 123.4 all-reduce.17
where the time goes:
time: 3660 us; the launch traced here: 3640 us
  waiting for transfers between devices  1610 us (44%)
  other arithmetic  890 us (24%)
  matrix products  522 us (14%)
  blocking collectives  311 us (8%)
  local copies, waits for them, and re-layouts  281 us (8%)
    reduce_scatter x1, waiting for transfers between devices, on_device(): lax.psum_scatter(grad_in_proj.astype(jnp.bfloat16), 'shard', scatter_dime...  542 us
    all_gather x1, waiting for transfers between devices, on_device(): lax.all_gather(in_proj, 'shard', axis=0, tiled=True)  400 us
    another operation x48, other arithmetic, selective_block_step(): summed = jnp.cumsum(jnp.exp(-exponent) * feeding, axis=0)  352 us
    dot_general x32, matrix products, selective_block_step(): emitted = jnp.einsum('qn,qne->qe', output_block, states, precision=HIGHEST)  327 us
    reduce_scatter x1, waiting for transfers between devices, on_device(): lax.psum_scatter(grad_out_proj.astype(jnp.bfloat16), 'shard', scatter_dim...  255 us
    reduce_sum x16, other arithmetic, selective_block_step(): exponent = rates[None, :, :] * running[:, None, :]  196 us
    all_gather x1, waiting for transfers between devices, on_device(): lax.all_gather(out_proj, 'shard', axis=0, tiled=True)  192 us
    psum x1, waiting for transfers between devices, on_device(): lax.psum(shares[1].astype(jnp.bfloat16), 'rep').astype(jnp.float32)  112 us
  transfers between devices with their start and end apart: 16, of which 8 were waited for; matrix products, arithmetic and copies ran while one was open for 17% of the time, Pallas kernels for 0%

commit v1 on v0

--- a/solution.py
+++ b/solution.py
@@ -7,6 +7,24 @@
 STRETCH = 32
 EPSILON = 1e-05
 HIGHEST = lax.Precision.HIGHEST
+
+
+def collect(shard, axis, dim):
+    ways, here, turn = (lax.axis_size(axis), lax.axis_index(axis), shard.shape[dim])
+    dims = [n * ways if d == dim else n for d, n in enumerate(shard.shape)]
+    full = lax.dynamic_update_slice_in_dim(
+        jnp.zeros(dims, shard.dtype), shard, here * turn, axis=dim
+    )
+    going_up = going_down = shard
+    for far in range(1, ways // 2 + 1):
+        going_up = lax.ppermute(going_up, axis, [(d, (d + 1) % ways) for d in range(ways)])
+        full = lax.dynamic_update_slice_in_dim(full, going_up, (here - far) % ways * turn, axis=dim)
+        if 2 * far < ways:
+            going_down = lax.ppermute(going_down, axis, [(d, (d - 1) % ways) for d in range(ways)])
+            full = lax.dynamic_update_slice_in_dim(
+                full, going_down, (here + far) % ways * turn, axis=dim
+            )
+    return full
 
 
 def shifted(value, axis, steps):
@@ -183,7 +201,7 @@
     valid_rows = (places < slot_len).astype(jnp.float32)[:, None]
     gathered = (
         lax.all_gather(norm_gain, "shard", axis=0, tiled=True),
-        lax.all_gather(in_proj, "shard", axis=0, tiled=True),
+        collect(in_proj, "shard", 0),
         lax.all_gather(conv_weight, "shard", axis=1, tiled=True),
         lax.all_gather(conv_bias, "shard", axis=0, tiled=True),
         lax.all_gather(x_proj, "shard", axis=0, tiled=True),

time: 3660 us -> 4380 us (1.20)
  waiting for transfers between devices: 1610 us -> 2220 us
  starting transfers between devices: 5.44 us -> 58.5 us
    ppermute x0 -> x7, waiting for transfers between devices: none -> 553 us  [the longest x4 463 us: collect(): lax.ppermute(going_up, axis, [(d, (d + 1) % ways) for d in range(ways)])]
    all_gather x1, waiting for transfers between devices: 400 us -> 638 us  [on_device(): lax.all_gather(in_proj, 'shard', axis=0, tiled=True)]
    all_gather x1, waiting for transfers between devices: 192 us -> 0.02 us  [on_device(): lax.all_gather(out_proj, 'shard', axis=0, tiled=True)]
    all_gather x1, blocking collectives: 62.7 us -> 139 us  [on_device(): lax.all_gather(norm_gain, 'shard', axis=0, tiled=True)]
    reduce_scatter x1, waiting for transfers between devices: 0.01 us -> 68.2 us  [on_device(): lax.psum_scatter(grad_x_proj.astype(jnp.bfloat16), 'shard', scatter_dimen...]
    reduce_scatter x1, waiting for transfers between devices: 63.6 us -> 4.63 us  [on_device(): lax.psum_scatter(grad_a_log.astype(jnp.bfloat16), 'shard', scatter_dimens...]
    ppermute x0 -> x7, starting transfers between devices: none -> 54.2 us  [the longest x3 46.2 us: collect(): lax.ppermute(going_down, axis, [(d, (d - 1) % ways) for d in range(ways)])]
  transfers between devices with their start and end apart: 16 -> 23, of which waited for: 8 -> 10; matrix products, arithmetic and copies ran while one was open for 17% -> 15% of each run, Pallas kernels for 0% -> 0%
where the time goes in v1:
time: 4380 us; the launch traced here: 4370 us
  waiting for transfers between devices  2220 us (51%)
  other arithmetic  896 us (20%)
  matrix products  518 us (12%)
  blocking collectives  326 us (7%)
  local copies, waits for them, and re-layouts  324 us (7%)
  starting transfers between devices  58.5 us (1%)
    all_gather x1, waiting for transfers between devices, on_device(): lax.all_gather(in_proj, 'shard', axis=0, tiled=True)  638 us
    reduce_scatter x1, waiting for transfers between devices, on_device(): lax.psum_scatter(grad_in_proj.astype(jnp.bfloat16), 'shard', scatter_dime...  542 us
    ppermute x4, waiting for transfers between devices, collect(): lax.ppermute(going_up, axis, [(d, (d + 1) % ways) for d in range(ways)])  463 us
    another operation x48, other arithmetic, selective_block_step(): summed = jnp.cumsum(jnp.exp(-exponent) * feeding, axis=0)  353 us
    dot_general x32, matrix products, selective_block_step(): emitted = jnp.einsum('qn,qne->qe', output_block, states, precision=HIGHEST)  327 us
    reduce_scatter x1, waiting for transfers between devices, on_device(): lax.psum_scatter(grad_out_proj.astype(jnp.bfloat16), 'shard', scatter_dim...  283 us
    reduce_sum x16, other arithmetic, selective_block_step(): exponent = rates[None, :, :] * running[:, None, :]  196 us
    all_gather x1, blocking collectives, on_device(): lax.all_gather(norm_gain, 'shard', axis=0, tiled=True)  139 us
  transfers between devices with their start and end apart: 23, of which 10 were waited for; matrix products, arithmetic and copies ran while one was open for 15% of the time, Pallas kernels for 0%

profile of v1, /device:TPU:0, one launch (start us, length us, event | category | flops | bytes accessed | tf_op | source)
XLA Modules:
  0.0 4367.5 jit_solution(18370086742717236457)
XLA Ops:
  14.1 227.2 %collective-permute-done = bf16[256,8192]{1,0:T(8,128)(2,1)} collective-permute-done((bf16[256,8192]{1,0:T(8,128)(2,1)}, bf16[256,8192]{1,0:T(8,128)(2,1)}, u32[]{:S(2)}, u32[]{:S(2)}) %collective-permute-start) | collective-permute-done | bytes 4194336 | tf_op jit(solution)/shard_map/ppermute | solution.py:20
  247.0 236.1 %collective-permute-done.2 = bf16[256,8192]{1,0:T(8,128)(2,1)} collective-permute-done((bf16[256,8192]{1,0:T(8,128)(2,1)}, bf16[256,8192]{1,0:T(8,128)(2,1)}, u32[]{:S(2)}, u32[]{:S(2)}) %collective-permute-start.2) | collective-permute-done | bytes 4194336 | tf_op jit(solution)/shard_map/ppermute | solution.py:20
  486.6 138.7 %all-gather.4 = bf16[8,1,256]{2,1,0:T(2,128)(2,1)S(1)} all-gather(bf16[1,1,256]{2,1,0:T(2,128)(2,1)S(1)} %reshape.226), channel_id=1, replica_groups=mesh['rep'=4,'shard'=8] {'shard'}, dimensions={0}, use_global_device_ids=true | all-gather | bytes 4608 | tf_op jit(solution)/shard_map/all_gather | solution.py:203
  626.0 26.2 all-gather.3
  652.9 26.1 all-gather.6
  680.3 26.1 all-gather.5
  706.5 30.7 all_gather.55
  737.3 31.1 all_gather.53
  787.1 40.0 collective-permute-start.5
  850.1 89.9 %collective-permute-done.5 = bf16[256,8192]{1,0:T(8,128)(2,1)S(1)} collective-permute-done((bf16[256,8192]{1,0:T(8,128)(2,1)}, bf16[256,8192]{1,0:T(8,128)(2,1)S(1)}, u32[]{:S(2)}, u32[]{:S(2)}) %collective-permute-start.5) | collective-permute-done | bytes 4194336 | tf_op jit(solution)/shard_map/ppermute | solution.py:23
  944.5 26.9 fusion.92
  980.8 32.6 multiply_reduce_fusion.6
  1035.1 78.1 %while.94 = (s32[]{:T(128)}, f32[16,4096]{1,0:T(8,128)S(1)}, f32[16,32,4096]{2,1,0:T(8,128)}, f32[16,4096]{1,0:T(8,128)S(1)}, f32[16,32,4096]{2,1,0:T(8,128)}, /...) while((s32[]{:T(128)}, f32[16,4096]{1,0:T(8,128)S(1)}, ...), condition=%wide.region_6.7_spmd.clone, body=%wide.region_3.6_spmd.clone.sunk | while | flops 12910595 | bytes 7415935 | solution.py:114
  1115.4 60.5 %while.96 = (s32[]{:T(128)}, f32[16,4096]{1,0:T(8,128)S(1)}, f32[4096]{0:T(1024)S(1)}, f32[16,4096]{1,0:T(8,128)S(1)}, f32[16,32,4096]{2,1,0:T(8,128)}, /*index=...) while((s32[]{:T(128)}, f32[16,4096]{1,0:T(8,128)S(1)}, ...), condition=%wide.region_16.17_spmd.clone, body=%wide.region_13.16_spmd.clone.sunk | while | flops 12648451 | bytes 6613123 | solution.py:139
  1191.4 277.8 %while.93 = (s32[]{:T(128)}, f32[16,4096]{1,0:T(8,128)S(1)}, f32[16,32,4096]{2,1,0:T(8,128)}, f32[16,16,4096]{2,1,0:T(8,128)}, f32[1,16,4096]{2,1,0:T(8,128)S(1)...) while((s32[]{:T(128)}, f32[16,4096]{1,0:T(8,128)S(1)}, ...), condition=%wide.region_12.13_spmd, body=%wide.region_9.12_spmd.sunk | while | flops 109051904 | bytes 58212524 | solution.py:87
  1488.7 964.5 %while.98 = (s32[]{:T(128)}, f32[16,4096]{1,0:T(8,128)}, f32[16,4096]{1,0:T(8,128)S(1)}, f32[16,32,4096]{2,1,0:T(8,128)}, f32[16,32,4096]{2,1,0:T(8,128)}, /*ind...) while((s32[]{:T(128)}, f32[16,4096]{1,0:T(8,128)}, ...), condition=%wide.region_29.30_spmd.clone, body=%wide.region_19.29_spmd.clone.sunk | while | flops 243269120 | bytes 81833296 | solution.py:87
  1559.9 15.1 fusion.135
  1620.2 15.1 fusion.135
  1680.5 15.1 fusion.135
  1740.7 15.1 fusion.135
  1801.0 15.1 fusion.135
  1861.2 15.1 fusion.135
  2465.8 29.4 multiply_reduce_fusion.9
  2554.5 25.6 convolution_convert_fusion
  2599.2 27.8 reduce-scatter.13.cloned.1.call-done
  2627.0 68.2 %reduce-scatter.11.cloned.1.call-done = bf16[512,160]{0,1:T(8,128)(2,1)} async-done(((bf16[4096,160]{0,1:T(8,128)(2,1)}), bf16[512,160]{0,1:T(8,128)(2,1)}) %reduce-scatter.11.cloned.1.call-update) | async-done | bytes 163856 | tf_op jit(solution)/shard_map/reduce_scatter | solution.py:345
  2695.1 282.9 %reduce-scatter.17.cloned.1.call-done = bf16[512,2048]{1,0:T(8,128)(2,1)} async-done(((bf16[4096,2048]{1,0:T(8,128)(2,1)}), bf16[512,2048]{1,0:T(8,128)(2,1)}) %reduce-scatter.17.cloned.1.call-update) | async-done | bytes 2097168 | tf_op jit(solution)/shard_map/reduce_scatter | solution.py:360
  2978.0 541.6 %reduce-scatter.9.cloned.1.call-done = bf16[256,8192]{1,0:T(8,128)(2,1)} async-done(((bf16[2048,8192]{1,0:T(8,128)(2,1)}), bf16[256,8192]{1,0:T(8,128)(2,1)}) %reduce-scatter.9.cloned.1.call-update) | async-done | bytes 4194320 | tf_op jit(solution)/shard_map/reduce_scatter | solution.py:336
  3519.7 638.1 %all-gather.21.cloned.1.call-done = bf16[2048,8192]{1,0:T(8,128)(2,1)} async-done(((bf16[256,8192]{1,0:T(8,128)(2,1)}), bf16[2048,8192]{1,0:T(8,128)(2,1)}) %all-gather.21.cloned.1.call-update) | async-done | bytes 33554448 | tf_op jit(solution)/shard_map/all_gather | solution.py:279
  4157.8 25.3 fusion.61
  4183.1 35.9 all-reduce.13
  4244.6 105.4 %all-reduce.18.cloned.1.call-done = (bf16[256,8192]{1,0:T(8,128)(2,1)}, bf16[512,160]{0,1:T(8,128)(2,1)}, bf16[128,512]{1,0:T(8,128)(2,1)}, bf16[512,2048]{1,0:T(8,128)(2,1)}) async-done(((bf16[256,8192]{1,0:T(8,128)(2,1)}, bf16[512,160]{0,1:T(8,128)(2,1)}, bf16[128,512]{1,0:T(8,128)(2,1)}, bf16[512,2048]{1,0:T(8,128)(2,1)}), (bf16[256,8192]{1,0:T(8,128)(2,1)}, bf16[512,160]{0,1:T(8,128)(2,1)}, ...) | async-done | bytes 6586384 | tf_op jit(solution)/shard_map/psum | solution.py:366
  (1133 shorter events, 1563.8 us)
Async XLA Ops:
  7.2 973.5 %all-gather.19.cloned.1.call-start = ((), (), s32[]{:S(2)}) async-start(), calls=%async_computation.8 | async-start | bytes 18874368 | tf_op jit(solution)/shard_map/all_gather | solution.py:212
  7.9 1005.5 %all-gather.15.cloned.1.call-start = ((), (), s32[]{:S(2)}) async-start(), calls=%async_computation.6 | async-start | bytes 1474560 | tf_op jit(solution)/shard_map/all_gather | solution.py:207
  8.0 233.4 %collective-permute-start = (bf16[256,8192]{1,0:T(8,128)(2,1)}, bf16[256,8192]{1,0:T(8,128)(2,1)}, u32[]{:S(2)}, u32[]{:S(2)}) collective-permute-start(bf16[256,8192]{1,0:T(8,128)(2,1)} %param.31), channel_id=1, source_target_pairs={{0,1},{1,2},{2,3},{3,4},{4,5},{5,6},{6,7},{7,0},{8,9},{9,10},{10,1... | collective-permute-start | bytes 12582920 | tf_op jit(solution)/shard_map/ppermute | solution.py:20
  11.0 232.9 %collective-permute-start.1 = (bf16[256,8192]{1,0:T(8,128)(2,1)}, bf16[256,8192]{1,0:T(8,128)(2,1)}, u32[]{:S(2)}, u32[]{:S(2)}) collective-permute-start(bf16[256,8192]{1,0:T(8,128)(2,1)} %param.31), channel_id=1, source_target_pairs={{0,7},{1,0},{2,1},{3,2},{4,3},{5,4},{6,5},{7,6},{8,15},{9,8},{10,9... | collective-permute-start | bytes 12582920 | tf_op jit(solution)/shard_map/ppermute | solution.py:23
  241.3 241.8 %collective-permute-start.2 = (bf16[256,8192]{1,0:T(8,128)(2,1)}, bf16[256,8192]{1,0:T(8,128)(2,1)}, u32[]{:S(2)}, u32[]{:S(2)}) collective-permute-start(bf16[256,8192]{1,0:T(8,128)(2,1)} %collective-permute-done), channel_id=1, source_target_pairs={{0,1},{1,2},{2,3},{3,4},{4,5},{5,6},{6,7},{7,0},{8,9},{9,10},{10,1... | collective-permute-start | bytes 12582920 | tf_op jit(solution)/shard_map/ppermute | solution.py:20
  243.8 773.7 %all-gather.17.cloned.1.call-start = ((), (), s32[]{:S(2)}) async-start(), calls=%async_computation.7 | async-start | bytes 1179648 | tf_op jit(solution)/shard_map/all_gather | solution.py:208
  243.9 543.2 %collective-permute-start.3 = (bf16[256,8192]{1,0:T(8,128)(2,1)}, bf16[256,8192]{1,0:T(8,128)(2,1)}, u32[]{:S(2)}, u32[]{:S(2)}) collective-permute-start(bf16[256,8192]{1,0:T(8,128)(2,1)} %collective-permute-done.1), channel_id=1, source_target_pairs={{0,7},{1,0},{2,1},{3,2},{4,3},{5,4},{6,5},{7,6},{8,15},{9,8},{10,9... | collective-permute-start | bytes 12582920 | tf_op jit(solution)/shard_map/ppermute | solution.py:23
  483.2 348.5 %collective-permute-start.4 = (bf16[256,8192]{1,0:T(8,128)(2,1)}, bf16[256,8192]{1,0:T(8,128)(2,1)}, u32[]{:S(2)}, u32[]{:S(2)}) collective-permute-start(bf16[256,8192]{1,0:T(8,128)(2,1)} %collective-permute-done.2), channel_id=1, source_target_pairs={{0,1},{1,2},{2,3},{3,4},{4,5},{5,6},{6,7},{7,0},{8,9},{9,10},{10,1... | collective-permute-start | bytes 12582920 | tf_op jit(solution)/shard_map/ppermute | solution.py:20
  485.7 691.2 %all-gather.23.cloned.1.call-start = ((), (), s32[]{:S(2)}) async-start(), calls=%async_computation.15 | async-start | bytes 2359296 | tf_op jit(solution)/shard_map/all_gather | solution.py:38
  625.3 319.2 %copy-start.29 = (f32[8,1,256]{2,1,0:T(1,128)}, f32[8,1,256]{2,1,0:T(1,128)S(1)}, u32[]{:S(2)}) copy-start(f32[8,1,256]{2,1,0:T(1,128)S(1)} %convert_element_type.193) | copy-start | bytes 24580
  706.5 311.1 %copy-start.26 = (f32[8,1,512]{2,1,0:T(1,128)}, f32[8,1,512]{2,1,0:T(1,128)S(1)}, u32[]{:S(2)}) copy-start(f32[8,1,512]{2,1,0:T(1,128)S(1)} %convert_element_type.194) | copy-start | bytes 49156
  768.4 259.3 %copy-start.15 = (bf16[16,4096]{1,0:T(8,128)(2,1)}, bf16[16,4096]{1,0:T(8,128)(2,1)S(1)}, u32[]{:S(2)}) copy-start(bf16[16,4096]{1,0:T(8,128)(2,1)S(1)} %all_gather.53) | copy-start | bytes 393220
  787.1 152.9 %collective-permute-start.5 = (bf16[256,8192]{1,0:T(8,128)(2,1)}, bf16[256,8192]{1,0:T(8,128)(2,1)S(1)}, u32[]{:S(2)}, u32[]{:S(2)}) collective-permute-start(bf16[256,8192]{1,0:T(8,128)(2,1)} %collective-permute-done.3), channel_id=1, source_target_pairs={{0,7},{1,0},{2,1},{3,2},{4,3},{5,4},{6,5},{7,6},{8,15},{9,8},{10,9... | collective-permute-start | bytes 12582920 | tf_op jit(solution)/shard_map/ppermute | solution.py:23
  831.7 110.6 %collective-permute-start.6 = (bf16[256,8192]{1,0:T(8,128)(2,1)}, bf16[256,8192]{1,0:T(8,128)(2,1)S(1)}, u32[]{:S(2)}, u32[]{:S(2)}) collective-permute-start(bf16[256,8192]{1,0:T(8,128)(2,1)} %collective-permute-done.4), channel_id=1, source_target_pairs={{0,1},{1,2},{2,3},{3,4},{4,5},{5,6},{6,7},{7,0},{8,9},{9,10},{10,1... | collective-permute-start | bytes 12582920 | tf_op jit(solution)/shard_map/ppermute | solution.py:20
  972.3 8.3 collective-permute-start.7
  1028.5 148.4 %all-gather.25.cloned.1.call-start = ((), (), s32[]{:S(2)}) async-start(), calls=%async_computation.16 | async-start | bytes 2359296 | tf_op jit(solution)/shard_map/all_gather | solution.py:38
  1115.0 354.2 %all-gather.27.cloned.1.call-start = ((), (), s32[]{:S(2)}) async-start(), calls=%async_computation.17 | async-start | bytes 2359296 | tf_op jit(solution)/shard_map/all_gather | solution.py:38
  1176.8 1421.4 %reduce-scatter.19.cloned.1.call-start = ((), (), s32[]{:S(2)}) async-start(), calls=%async_computation.18 | async-start | bytes 1179648
  1191.4 277.8 %copy-start.1 = (f32[16,4096]{1,0:T(8,128)S(1)}, f32[16,4096]{1,0:T(8,128)}, u32[]{:S(2)}) copy-start(f32[16,4096]{1,0:T(8,128)} %custom-call.3) | copy-start | bytes 786436
  1488.7 965.6 %copy-start.27 = (f32[8,1,512]{2,1,0:T(1,128)S(1)}, f32[8,1,512]{2,1,0:T(1,128)}, u32[]{:S(2)}) copy-start(f32[8,1,512]{2,1,0:T(1,128)} %copy-done.26) | copy-start | bytes 49156
  2496.6 130.3 %reduce-scatter.13.cloned.1.call-start = ((), (), s32[]{:S(2)}) async-start(), calls=%async_computation.12 | async-start | bytes 1179648 | tf_op jit(solution)/shard_map/reduce_scatter | solution.py:348
  2500.6 194.5 %reduce-scatter.11.cloned.1.call-start = ((), (), s32[]{:S(2)}) async-start(), calls=%async_computation.11 | async-start | bytes 1474560 | tf_op jit(solution)/shard_map/reduce_scatter | solution.py:345
  2504.8 473.2 %reduce-scatter.17.cloned.1.call-start = ((), (), s32[]{:S(2)}) async-start(), calls=%async_computation.14 | async-start | bytes 18874368 | tf_op jit(solution)/shard_map/reduce_scatter | solution.py:360
  2533.6 986.0 %reduce-scatter.9.cloned.1.call-start = ((), (), s32[]{:S(2)}) async-start(), calls=%async_computation.10 | async-start | bytes 37748736 | tf_op jit(solution)/shard_map/reduce_scatter | solution.py:336
  2534.9 17.7 collective-permute-start.8
  2580.0 1577.8 %all-gather.21.cloned.1.call-start = ((), (), s32[]{:S(2)}) async-start(), calls=%async_computation.9 | async-start | bytes 37748736 | tf_op jit(solution)/shard_map/all_gather | solution.py:279
  2580.6 1643.4 %reduce-scatter.15.cloned.1.call-start = ((), (), s32[]{:S(2)}) async-start(), calls=%async_computation.13 | async-start | bytes 147456 | tf_op jit(solution)/shard_map/reduce_scatter | solution.py:354
  2583.3 1766.6 %all-reduce.18.cloned.1.call-start = ((), (), s32[]{:S(2)}) async-start(), calls=%async_computation.19 | async-start | bytes 13172736 | tf_op jit(solution)/shard_map/psum | solution.py:366
  3519.6 663.5 %copy-start.28 = (bf16[4096]{0:T(1024)(128)(2,1)S(1)}, bf16[4096]{0:T(1024)(128)(2,1)}, u32[]{:S(2)}) copy-start(bf16[4096]{0:T(1024)(128)(2,1)} %get-tuple-element.1054) | copy-start | bytes 24580
  3519.6 663.4 %copy-start.39 = (bf16[4096]{0:T(1024)(128)(2,1)S(1)}, bf16[4096]{0:T(1024)(128)(2,1)}, u32[]{:S(2)}) copy-start(bf16[4096]{0:T(1024)(128)(2,1)} %get-tuple-element.1050) | copy-start | bytes 24580
  3519.7 663.4 %copy-start.40 = (bf16[4096]{0:T(1024)(128)(2,1)S(1)}, bf16[4096]{0:T(1024)(128)(2,1)}, u32[]{:S(2)}) copy-start(bf16[4096]{0:T(1024)(128)(2,1)} %get-tuple-element.940) | copy-start | bytes 24580
  3519.7 718.8 %copy-start.41 = (f32[512]{0:T(512)S(1)}, f32[512]{0:T(512)}, u32[]{:S(2)}) copy-start(f32[512]{0:T(512)} %get-tuple-element.1083) | copy-start | bytes 6148
  (116 other events, 2410.2 us)
Sparse Core Ops, SparseCore 0:
  10.1 495.0 all-gather.18
  507.3 70.3 all-gather.14
  579.7 53.7 all-gather.16
  1028.6 48.1 all-gather.22
  1115.1 48.2 all-gather.24
  1176.9 48.2 all-gather.26
  2496.7 63.1 reduce-scatter.18
  2563.3 63.6 reduce-scatter.12
  2630.4 64.6 reduce-scatter.10
  2698.7 279.1 reduce-scatter.16
  2981.8 537.7 reduce-scatter.8
  3521.0 636.7 all-gather.20
  4161.7 62.2 reduce-scatter.14
  4226.4 123.5 all-reduce.17
